TPU v7x, 256 devices: a whole 4x4x8 slice. The times are simulated.
256 devices in a mesh: expert: 8 (over x_hi, y), dp: 32 (over x_lo, z, core).
Axes of the slice: x: 4 (x_hi: 2, x_lo: 2; x = x_hi * 2 + x_lo), y: 4, z: 8, core: 2. Of those that a mesh axis runs over, the one named last changes fastest.
Arguments:
- tokens: bfloat16 [2048, 4096], P(('expert', 'dp')), may hold values from -6 to 6
- routes: int32 [2048, 2], P(('expert', 'dp')), may hold values from 0 to 7, all different within a row; in each aligned block of 8 rows (0 to 7, 8 to 15, ...) at most 3 rows name the same one
- route_weights: float32 [2048, 2], P(('expert', 'dp')), may hold values from 0.2 to 1
- w_gate: bfloat16 [8, 4096, 14336], P('expert', None, 'dp'), may hold values from -0.09375 to 0.09375
- w_up: bfloat16 [8, 4096, 14336], P('expert', None, 'dp'), may hold values from -0.09375 to 0.09375
- w_down: bfloat16 [8, 14336, 4096], P('expert', 'dp'), may hold values from -0.046875 to 0.046875
Outputs:
- mixed: bfloat16 [2048, 4096], P(('expert', 'dp'))
Inputs may be any that keep to these rules, and one draw needn't show every extreme that they name: `routes`: within the rows of one device (aligned blocks of 8 rows) the two experts of a token differ and no expert is named more than 3 times; in every draw some block names some expert exactly 3 times. Every expert is named somewhere.
All inputs are finite; a program needn't handle non-finite values.
Results may differ from a plain program's by a relative error of at most 0.0057.
Values may be sent and summed in bfloat16 or wider, within the bound.
No kernel may reach another device: no remote copies, remote signals or barrier semaphores. Data moves between devices by JAX's collectives and lax.ppermute only.
A program may use at most 128 MiB of HBM per device.

v0:
```python
import jax
import jax.numpy as jnp
from jax import lax
from jax.sharding import PartitionSpec as P


def expert_projection(gate_local, up_local, down_local):

    def project(block_rows, first_row):
        gated = jnp.dot(block_rows, gate_local, preferred_element_type=jnp.float32)
        upward = jnp.dot(block_rows, up_local, preferred_element_type=jnp.float32)
        hidden = (jax.nn.silu(gated) * upward).astype(jnp.bfloat16)
        return jnp.dot(hidden, down_local, preferred_element_type=jnp.float32)

    return project


def local(tokens, routes, route_weights, w_gate, w_up, w_down):
    groups = lax.axis_size("expert")
    tok_count = tokens.shape[0]
    features = tokens.shape[1]
    capacity = 3 * tok_count // groups
    columns = groups * capacity
    listed = routes.reshape(2 * tok_count)
    chosen = (listed[:, None] == jnp.arange(groups, dtype=jnp.int32)[None, :]).astype(jnp.int32)
    before = jnp.cumsum(chosen, axis=0) - chosen
    column = listed * capacity + jnp.sum(before * chosen, axis=1)
    placing = (column[:, None] == jnp.arange(columns, dtype=jnp.int32)[None, :]).astype(
        jnp.bfloat16
    )
    placing = placing.reshape(tok_count, 2, columns)
    sending = jnp.sum(placing, axis=1)
    outgoing = jnp.einsum("tw,td->wd", sending, tokens, preferred_element_type=jnp.float32).astype(
        jnp.bfloat16
    )
    arrived = lax.all_to_all(
        outgoing.reshape(groups, capacity, features),
        "expert",
        split_axis=0,
        concat_axis=0,
        tiled=True,
    )
    arrived = arrived.reshape(columns, features)
    project = expert_projection(w_gate[0], w_up[0], w_down[0])
    partials = project(lax.all_gather(arrived, "dp", axis=0, tiled=True), jnp.int32(0))
    summed = lax.psum_scatter(partials, "dp", scatter_dimension=0, tiled=True)
    results = summed.astype(jnp.bfloat16).reshape(groups, capacity, features)
    returned = lax.all_to_all(results, "expert", split_axis=0, concat_axis=0, tiled=True).reshape(
        columns, features
    )
    picked = jnp.einsum("tkw,wd->tkd", placing, returned, preferred_element_type=jnp.float32)
    combined = jnp.sum(route_weights[:, :, None] * picked, axis=1)
    return combined.astype(jnp.bfloat16)


def solution(mesh):
    placed = (
        P(("expert", "dp"), None),
        P(("expert", "dp"), None),
        P(("expert", "dp"), None),
        P("expert", None, "dp"),
        P("expert", None, "dp"),
        P("expert", "dp", None),
    )
    return jax.shard_map(
        local, mesh=mesh, in_specs=placed, out_specs=P(("expert", "dp"), None), check_vma=False
    )
```

profile of v0, /device:TPU:8, one launch (start us, length us, event | category | flops | bytes accessed | tf_op | source)
XLA Modules:
  0.0 278.0 jit_solution(10584551748539052171)
XLA Ops:
  6.5 0.8 copy.13
  7.3 0.1 eq.51
  7.4 0.1 fusion.16
  7.5 0.2 select_reduce_fusion
  7.7 0.1 reduce_sum.33
  7.8 0.1 copy.15
  7.9 0.1 fusion.20
  8.0 0.3 convolution_convert_fusion
  8.2 0.1 reshape.54
  8.4 14.1 %all_to_all.10 = bf16[8,3,4096]{2,1,0:T(4,128)(2,1)S(1)} all-to-all(bf16[8,3,4096]{2,1,0:T(4,128)(2,1)S(1)} %reshape.54), channel_id=1, replica_groups=mesh['expert'=8,'dp'=32] {'expert'}, dimensions={0} | all-to-all | bytes 393216 | tf_op jit(solution)/shard_map/all_to_all | solution.py:36
  22.5 0.8 reshape.55
  23.3 0.0 all-gather.2.cloned.1.call-update
  23.3 0.0 reduce-scatter.2.cloned.1.call-start
  23.4 69.3 %all-gather.2.cloned.1.call-done = bf16[768,4096]{1,0:T(8,128)(2,1)} async-done(((bf16[24,4096]{1,0:T(8,128)(2,1)}), bf16[768,4096]{1,0:T(8,128)(2,1)}) %all-gather.2.cloned.1.call-update) | async-done | bytes 6291472 | tf_op jit(solution)/shard_map/all_gather | solution.py:45
  92.6 6.9 %fusion.4 = f32[768,448]{0,1:T(8,128)S(1)} fusion(bf16[768,4096]{1,0:T(8,128)(2,1)} %all-gather.2.cloned.1.call-done, bf16[1,4096,448]{1,2,0:T(8,128)(2,1)} %param.9), kind=kOutput, calls=%fused_computation.6 | convolution fusion | flops 2818572288 | bytes 11337728 | tf_op jit(solution)/shard_map/dot_general | solution.py:10
  99.5 17.9 %fusion = f32[768,4096]{1,0:T(8,128)} fusion(bf16[1,448,4096]{2,1,0:T(8,128)(2,1)} %param.11, bf16[768,4096]{1,0:T(8,128)(2,1)} %all-gather.2.cloned.1.call-done, bf16[1,4096,448]{1,2,0:T(8,128)(2,1)} %param.10, f32[768,448]{0,1:T(8,128)S(1)} %fusion.4), kind=kOutput, calls=%fused_computation.2 | convolution fusion | flops 5639208960 | bytes 27590656 | tf_op jit(solution)/shard_map/dot_general | solution.py:13
  117.4 0.0 reduce-scatter.2.cloned.1.call-update
  117.4 137.9 %reduce-scatter.2.cloned.1.call-done = f32[24,4096]{1,0:T(8,128)} async-done(((f32[768,4096]{1,0:T(8,128)}), f32[24,4096]{1,0:T(8,128)}) %reduce-scatter.2.cloned.1.call-update) | async-done | bytes 393232 | tf_op jit(solution)/shard_map/reduce_scatter | solution.py:46
  255.4 1.0 convert_element_type.25
  256.4 0.1 reshape.56
  256.5 13.6 %all_to_all.11 = bf16[8,3,4096]{2,1,0:T(4,128)(2,1)S(1)} all-to-all(bf16[8,3,4096]{2,1,0:T(4,128)(2,1)S(1)} %reshape.56), channel_id=1, replica_groups=mesh['expert'=8,'dp'=32] {'expert'}, dimensions={0} | all-to-all | bytes 393216 | tf_op jit(solution)/shard_map/all_to_all | solution.py:48
  270.2 0.2 reshape.58
  270.3 0.0 copy-done.1
  270.3 0.9 fusion.12
  (6 shorter events, 0.1 us)
Async XLA Ops:
  6.5 1.4 copy-start
  6.5 86.1 %all-gather.2.cloned.1.call-start = ((), (), s32[]{:S(2)}) async-start(), calls=%async_computation.3 | async-start | bytes 6488064 | tf_op jit(solution)/shard_map/all_gather | solution.py:45
  23.3 232.0 %reduce-scatter.2.cloned.1.call-start = ((), (), s32[]{:S(2)}) async-start(), calls=%async_computation.4 | async-start | bytes 12976128 | tf_op jit(solution)/shard_map/reduce_scatter | solution.py:46
  117.4 152.9 %copy-start.1 = (f32[8,2]{0,1:T(2,128)S(1)}, f32[8,2]{0,1:T(2,128)}, u32[]{:S(2)}) copy-start(f32[8,2]{0,1:T(2,128)} %param.8) | copy-start | bytes 196
Sparse Core Ops, SparseCore 0:
  23.4 69.1 all-gather.1
  117.6 137.7 reduce-scatter.1
where the time goes:
time: 278 us
  waiting for transfers between devices  207 us (74%)
  blocking collectives  27.7 us (10%)
  matrix products  25.9 us (9%)
  between operations  13.5 us (5%)
    reduce_scatter x1, waiting for transfers between devices, local(): summed = lax.psum_scatter(partials, 'dp', scatter_dimension=0, tiled=True)  138 us
    all_gather x1, waiting for transfers between devices, local(): lax.all_gather(arrived, 'dp', axis=0, tiled=True)  69.3 us
    dot_general x1, matrix products, project(): return jnp.dot(hidden, down_local, preferred_element_type=jnp.float32)  17.9 us
    all_to_all x1, blocking collectives, local(): lax.all_to_all(outgoing.reshape(groups, capacity, features), 'expert', sp...  14.1 us
    all_to_all x1, blocking collectives, local(): lax.all_to_all(results, 'expert', split_axis=0, concat_axis=0, tiled=True)  13.6 us
    dot_general x1, matrix products, project(): gated = jnp.dot(block_rows, gate_local, preferred_element_type=jnp.float32)  6.9 us
  transfers between devices with their start and end apart: 2, of which 2 were waited for; matrix products, arithmetic and copies ran while one was open for 0% of the time, Pallas kernels for 0%

commit v1 on v0

--- a/solution.py
+++ b/solution.py
@@ -42,7 +42,12 @@
     )
     arrived = arrived.reshape(columns, features)
     project = expert_projection(w_gate[0], w_up[0], w_down[0])
-    partials = project(lax.all_gather(arrived, "dp", axis=0, tiled=True), jnp.int32(0))
+    partials = project(
+        jnp.concatenate(
+            lax.all_to_all(jnp.stack([arrived] * lax.axis_size("dp")), "dp", 0, 0), axis=0
+        ),
+        jnp.int32(0),
+    )
     summed = lax.psum_scatter(partials, "dp", scatter_dimension=0, tiled=True)
     results = summed.astype(jnp.bfloat16).reshape(groups, capacity, features)
     returned = lax.all_to_all(results, "expert", split_axis=0, concat_axis=0, tiled=True).reshape(

time: 278 us -> 353 us (1.27)
  blocking collectives: 27.7 us -> 178 us
  waiting for transfers between devices: 207 us -> 133 us
  matrix products: 25.9 us -> 22 us
    all_to_all x0 -> x1, blocking collectives: none -> 150 us  [local(): lax.all_to_all(jnp.stack([arrived] * lax.axis_size('dp')), 'dp', 0, 0)]
    all_gather x1 -> x0, waiting for transfers between devices: 69.3 us -> none  [local(): lax.all_gather(arrived, 'dp', axis=0, tiled=True)]
    reduce_scatter x1, waiting for transfers between devices: 138 us -> 133 us  [local(): summed = lax.psum_scatter(partials, 'dp', scatter_dimension=0, tiled=True)]
    dot_general x1, matrix products: 6.9 us -> 3.06 us  [project(): gated = jnp.dot(block_rows, gate_local, preferred_element_type=jnp.float32)]
  transfers between devices with their start and end apart: 2 -> 1, of which waited for: 2 -> 1; matrix products, arithmetic and copies ran while one was open for 0% -> 0% of each run, Pallas kernels for 0% -> 0%
where the time goes in v1:
time: 353 us
  blocking collectives  178 us (50%)
  waiting for transfers between devices  133 us (38%)
  matrix products  22 us (6%)
  between operations  13.5 us (4%)
  local copies, waits for them, and re-layouts  5.01 us (1%)
    all_to_all x1, blocking collectives, local(): lax.all_to_all(jnp.stack([arrived] * lax.axis_size('dp')), 'dp', 0, 0)  150 us
    reduce_scatter x1, waiting for transfers between devices, local(): summed = lax.psum_scatter(partials, 'dp', scatter_dimension=0, tiled=True)  133 us
    dot_general x1, matrix products, project(): return jnp.dot(hidden, down_local, preferred_element_type=jnp.float32)  17.9 us
    all_to_all x1, blocking collectives, local(): lax.all_to_all(outgoing.reshape(groups, capacity, features), 'expert', sp...  14.1 us
    all_to_all x1, blocking collectives, local(): lax.all_to_all(results, 'expert', split_axis=0, concat_axis=0, tiled=True)  13.7 us
  transfers between devices with their start and end apart: 1, of which 1 were waited for; matrix products, arithmetic and copies ran while one was open for 0% of the time, Pallas kernels for 0%

profile of v1, /device:TPU:8, one launch (start us, length us, event | category | flops | bytes accessed | tf_op | source)
XLA Modules:
  0.0 352.9 jit_solution(3810686533255854404)
XLA Ops:
  6.5 0.8 copy.13
  7.3 0.1 eq.51
  7.4 0.1 fusion.16
  7.5 0.2 select_reduce_fusion
  7.7 0.1 reduce_sum.33
  7.8 0.1 copy.15
  7.9 0.1 fusion.20
  8.0 0.3 convolution_convert_fusion
  8.2 0.1 reshape.56
  8.4 14.1 %all_to_all.15 = bf16[8,3,4096]{2,1,0:T(4,128)(2,1)S(1)} all-to-all(bf16[8,3,4096]{2,1,0:T(4,128)(2,1)S(1)} %reshape.56), channel_id=1, replica_groups=mesh['expert'=8,'dp'=32] {'expert'}, dimensions={0} | all-to-all | bytes 393216 | tf_op jit(solution)/shard_map/all_to_all | solution.py:36
  22.5 0.2 stack_reshape.2
  22.6 0.8 stack.3
  23.4 0.0 copy-start.3
  23.4 149.8 %all_to_all.16 = bf16[32,24,4096]{2,1,0:T(8,128)(2,1)S(1)} all-to-all(bf16[32,24,4096]{2,1,0:T(8,128)(2,1)S(1)} %stack.3), channel_id=1, replica_groups=mesh['expert'=8,'dp'=32] {'dp'}, dimensions={0} | all-to-all | bytes 12582912 | tf_op jit(solution)/shard_map/all_to_all | solution.py:47
  173.2 2.6 copy-done.1
  175.8 3.1 fusion.4
  178.9 17.9 %fusion = f32[768,4096]{1,0:T(8,128)} fusion(bf16[1,448,4096]{2,1,0:T(8,128)(2,1)} %param.11, bf16[768,4096]{1,0:T(8,128)(2,1)} %bitcast.25, bf16[1,4096,448]{1,2,0:T(8,128)(2,1)} %param.10, f32[768,448]{0,1:T(8,128)S(1)} %fusion.4), kind=kOutput, calls=%fused_computation.2 | convolution fusion | flops 5639208960 | bytes 27590656 | tf_op jit(solution)/shard_map/dot_general | solution.py:13
  196.7 0.0 reduce-scatter.2.cloned.1.call-update
  196.8 133.4 %reduce-scatter.2.cloned.1.call-done = f32[24,4096]{1,0:T(8,128)} async-done(((f32[768,4096]{1,0:T(8,128)}), f32[24,4096]{1,0:T(8,128)}) %reduce-scatter.2.cloned.1.call-update) | async-done | bytes 393232 | tf_op jit(solution)/shard_map/reduce_scatter | solution.py:51
  330.2 1.0 convert_element_type.25
  331.2 0.1 reshape.58
  331.3 13.7 %all_to_all.17 = bf16[8,3,4096]{2,1,0:T(4,128)(2,1)S(1)} all-to-all(bf16[8,3,4096]{2,1,0:T(4,128)(2,1)S(1)} %reshape.58), channel_id=1, replica_groups=mesh['expert'=8,'dp'=32] {'expert'}, dimensions={0} | all-to-all | bytes 393216 | tf_op jit(solution)/shard_map/all_to_all | solution.py:53
  345.0 0.2 reshape.60
  345.2 0.9 fusion.12
  (9 shorter events, 0.1 us)
Async XLA Ops:
  6.5 1.4 copy-start
  6.5 323.6 %reduce-scatter.2.cloned.1.call-start = ((), (), s32[]{:S(2)}) async-start(), calls=%async_computation.4 | async-start | bytes 12976128 | tf_op jit(solution)/shard_map/reduce_scatter | solution.py:51
  23.4 152.4 %copy-start.3 = (bf16[1,4096,448]{1,2,0:T(8,128)(2,1)S(1)}, bf16[1,4096,448]{1,2,0:T(8,128)(2,1)}, u32[]{:S(2)}) copy-start(bf16[1,4096,448]{1,2,0:T(8,128)(2,1)} %param.9) | copy-start | bytes 11010052
  173.2 2.6 copy-start.1
  196.7 148.5 %copy-start.2 = (f32[8,2]{0,1:T(2,128)S(1)}, f32[8,2]{0,1:T(2,128)}, u32[]{:S(2)}) copy-start(f32[8,2]{0,1:T(2,128)} %param.8) | copy-start | bytes 196
Sparse Core Ops, SparseCore 0:
  196.9 133.2 reduce-scatter.1
